TPU v7x, 128 devices: a whole 4x4x4 slice. The times are simulated.
128 devices in a mesh: own: 16 (over y, z), red: 8 (over x, core).
Axes of the slice: x: 4, y: 4, z: 4, core: 2. Of those that a mesh axis runs over, the one named last changes fastest.
Arguments:
- amp_tiles: bfloat16 [8192, 128, 128], P(('own', 'red')), may hold values from -6 to 6
- int_tiles: bfloat16 [8192, 128, 128], P(('own', 'red')), may hold values from -0.0625 to 0.0625
- requests: int32 [16, 8, 16, 2, 8], P('own', 'red'), may hold values from -1 to 63, as said below
- tri_amp: int32 [512, 8, 64], P('own', 'red'), may hold values from 0 to 127, as said below
- tri_int: int32 [512, 8, 64], P('own', 'red'), may hold values from 0 to 127, as said below
- tri_count: int32 [512, 8], P('own', 'red'), may hold values from 1 to 64, as said below
Outputs:
- residual: float32 [512, 128, 128], P(('own', 'red'))
Inputs may be any that keep to these rules, and one draw needn't show every extreme that they name: -1 marks an empty slot and live slots come first; the live numbers in one row of 8 slots are distinct; every owner device has 8 live amplitude requests to some holder and 8 live integral requests to some holder. tri_amp[t, r, k] // 8 is a holder h and tri_amp[t, r, k] % 8 is below the number of live amplitude requests of the owner of t, on red index r, to h. `tri_int`: likewise for the integral requests. `tri_count`: on every owner and red index some residual tile has 64 live triples.
All inputs are finite; a program needn't handle non-finite values.
Results may differ from a plain program's by a relative error of at most 0.0003.
Values may be sent and summed in bfloat16 or wider, within the bound.
No kernel may reach another device: no remote copies, remote signals or barrier semaphores. Data moves between devices by JAX's collectives and lax.ppermute only.
A program may use at most 128 MiB of HBM per device.

v0:
```python
import math

import jax
import jax.numpy as jnp
from jax import lax
from jax.sharding import PartitionSpec as P


def select_tiles(store, wanted):
    clipped = jnp.clip(wanted, 0, store.shape[0] - 1)
    picked = store[clipped]
    return jnp.where((wanted >= 0)[:, :, None, None], picked, jnp.zeros((), store.dtype))


def contract_rows(got_amp, got_int, amp_pos, int_pos, counts):
    row_count, slot_count = amp_pos.shape
    received = got_amp.shape[0]
    tile_width = got_amp.shape[-1]
    block_rows = math.gcd(8, row_count)
    keep_mask = lax.broadcasted_iota(jnp.int32, (row_count, slot_count), 1) < counts[:, None]
    flat_amp = got_amp.reshape(received, tile_width * tile_width)
    flat_int = got_int.reshape(received, tile_width * tile_width)
    slot_iota = lax.broadcasted_iota(jnp.int32, (1, 1, received), 2)

    def one_block(operands):
        block_amp, block_int, block_keep = operands
        pick_amp = ((block_amp[:, :, None] == slot_iota) & block_keep[:, :, None]).astype(
            got_amp.dtype
        )
        pick_int = (block_int[:, :, None] == slot_iota).astype(got_int.dtype)
        left_tiles = jnp.einsum(
            "nkm,mx->nkx", pick_amp, flat_amp, preferred_element_type=jnp.float32
        ).astype(got_amp.dtype)
        right_tiles = jnp.einsum(
            "nkm,mx->nkx", pick_int, flat_int, preferred_element_type=jnp.float32
        ).astype(got_int.dtype)
        left_tiles = left_tiles.reshape(block_rows, slot_count, tile_width, tile_width)
        right_tiles = right_tiles.reshape(block_rows, slot_count, tile_width, tile_width)
        return jnp.einsum(
            "nkpc,nkqc->npq", left_tiles, right_tiles, preferred_element_type=jnp.float32
        )

    def in_blocks(values):
        return values.reshape((row_count // block_rows, block_rows) + values.shape[1:])

    product = lax.map(one_block, (in_blocks(amp_pos), in_blocks(int_pos), in_blocks(keep_mask)))
    return product.reshape(row_count, tile_width, tile_width)


def body(amp_tiles, int_tiles, requests, tri_amp, tri_int, tri_count):
    wanted = requests[0, 0]
    asked = lax.all_to_all(wanted, "own", split_axis=0, concat_axis=0, tiled=True)
    send_amp = select_tiles(amp_tiles, asked[:, 0])
    send_int = select_tiles(int_tiles, asked[:, 1])
    got_amp, got_int = (
        lax.all_to_all(send_amp, "own", split_axis=0, concat_axis=0, tiled=True),
        lax.all_to_all(send_int, "own", split_axis=0, concat_axis=0, tiled=True),
    )
    flat_amp = got_amp.reshape((-1,) + got_amp.shape[2:])
    flat_int = got_int.reshape((-1,) + got_int.shape[2:])
    amp_pos = tri_amp[:, 0]
    int_pos = tri_int[:, 0]
    counts = tri_count[:, 0]
    share = amp_pos.shape[0] // lax.axis_size("red")
    partial_sum = contract_rows(flat_amp, flat_int, amp_pos, int_pos, counts)
    total_sum = lax.psum(partial_sum, "red")
    return lax.dynamic_slice_in_dim(total_sum, lax.axis_index("red") * share, share, 0)


def solution(mesh):
    placed = (
        P(("own", "red"), None, None),
        P(("own", "red"), None, None),
        P("own", "red", None, None, None),
        P("own", "red", None),
        P("own", "red", None),
        P("own", "red"),
    )
    return jax.shard_map(
        body, mesh=mesh, in_specs=placed, out_specs=P(("own", "red"), None, None), check_vma=False
    )
```

profile of v0, /device:TPU:1, one launch (start us, length us, event | category | flops | bytes accessed | tf_op | source)
XLA Modules:
  0.0 400.0 jit_solution(17868745536821819180)
XLA Ops:
  6.5 0.9 copy.19
  7.5 14.8 %all_to_all.15 = s32[16,2,8]{2,1,0:T(2,128)S(1)} all-to-all(s32[16,2,8]{2,1,0:T(2,128)S(1)} %bitcast.88), channel_id=1, replica_groups=mesh['own'=16,'red'=8] {'own'}, dimensions={0} | all-to-all | bytes 2048 | tf_op jit(solution)/shard_map/all_to_all | solution.py:52
  22.4 0.1 copy.26
  22.5 0.1 reshape.93
  22.6 0.1 copy.25
  22.7 3.0 gather_fusion.1
  25.7 6.9 %copy_select_fusion = bf16[16,8,128,128]{3,1,2,0:T(8,128)(2,1)} fusion(bf16[16,8,128,128]{3,2,1,0:T(8,128)(2,1)} %bitcast.85, pred[16,8]{1,0:T(8,128)(4,1)S(1)} %copy.25), kind=kLoop, calls=%fused_computation.21 | loop fusion | flops 2097152 | bytes 8388736 | tf_op jit(solution)/shard_map/jit(_where)/select_n | solution.py:12
  32.5 4.7 %all-to-all-start.2 = ((bf16[16,8,128,128]{3,1,2,0:T(8,128)(2,1)}), bf16[16,8,128,128]{3,1,2,0:T(8,128)(2,1)}, u32[]{:S(2)}, u32[]{:S(2)}) async-start(bf16[16,8,128,128]{3,1,2,0:T(8,128)(2,1)} %copy_select_fusion), calls=%async_computation.2 | async-start | bytes 8388608 | tf_op jit(solution)/shard_map/all_to_all | solution.py:57
  37.3 0.1 copy.22
  37.4 0.1 reshape.85
  37.5 0.1 copy.21
  37.6 3.0 gather_fusion
  40.6 6.8 %copy_select_fusion.1 = bf16[16,8,128,128]{3,1,2,0:T(8,128)(2,1)} fusion(bf16[16,8,128,128]{3,2,1,0:T(8,128)(2,1)} %bitcast.86, pred[16,8]{1,0:T(8,128)(4,1)S(1)} %copy.21), kind=kLoop, calls=%fused_computation.22 | loop fusion | flops 2097152 | bytes 8388736 | tf_op jit(solution)/shard_map/jit(_where)/select_n | solution.py:12
  47.4 41.6 %all-to-all-done.2 = bf16[16,8,128,128]{3,1,2,0:T(8,128)(2,1)} async-done(((bf16[16,8,128,128]{3,1,2,0:T(8,128)(2,1)}), bf16[16,8,128,128]{3,1,2,0:T(8,128)(2,1)}, u32[]{:S(2)}, u32[]{:S(2)}) %all-to-all-start.2) | async-done | bytes 4194336 | tf_op jit(solution)/shard_map/all_to_all | solution.py:57
  89.0 5.5 %all-to-all-start.1 = ((bf16[16,8,128,128]{3,1,2,0:T(8,128)(2,1)}), bf16[16,8,128,128]{3,1,2,0:T(8,128)(2,1)}, u32[]{:S(2)}, u32[]{:S(2)}) async-start(bf16[16,8,128,128]{3,1,2,0:T(8,128)(2,1)} %copy_select_fusion.1), calls=%async_computation.1 | async-start | bytes 8388608 | tf_op jit(solution)/shard_map/all_to_all | solution.py:56
  94.5 0.2 all-reduce.2.cloned.1.call-start
  94.8 0.5 broadcast.105
  95.3 0.6 reduce.3
  95.9 0.1 lt.37
  96.0 0.1 iota_compare_fusion.3
  96.1 45.7 %all-to-all-done.1 = bf16[16,8,128,128]{3,1,2,0:T(8,128)(2,1)} async-done(((bf16[16,8,128,128]{3,1,2,0:T(8,128)(2,1)}), bf16[16,8,128,128]{3,1,2,0:T(8,128)(2,1)}, u32[]{:S(2)}, u32[]{:S(2)}) %all-to-all-start.1) | async-done | bytes 4194336 | tf_op jit(solution)/shard_map/all_to_all | solution.py:56
  141.8 178.1 %while.12 = (s32[]{:T(128)}, f32[4,8,128,128]{3,2,1,0:T(8,128)}, s32[4,8,64]{2,1,0:T(8,128)}, pred[4,8,64]{2,1,0:T(8,128)(4,1)S(1)}, bf16[128,16384]{1,0:T(8,128...) while((s32[]{:T(128)}, f32[4,8,128,128]{3,2,1,0:T(8,128)}, ...), condition=%wide.region_1.2_spmd.clone.clone, body=%wide.region_0.1_spmd.clone.clone.sunk | while | flops 6459424768 | bytes 143145056 | solution.py:46
  141.8 0.7 dynamic-slice_bitcast_fusion.5
  142.5 7.0 %convolution_convert_fusion.5 = bf16[8,64,16384]{2,1,0:T(8,128)(2,1)S(1)} fusion(bf16[128,16384]{1,0:T(8,128)(2,1)} %get-tuple-element.172, s32[8,64]{1,0:T(8,128)S(1)} %get-tuple-element.151, pred[8,64]{1,0:T(8,128)(4,1)S(1)} %dynamic-slice_bitcast_fusion.6), kind=kOutput, calls=%fused_computation.4.clone.1 | convolution fusion | flops 2156003328 | bytes 20974080 | tf_op jit(solution)/shard_map/while/body/eval_jaxpr/nkm,mx->nkx/dot_general | solution.py:31
  149.5 8.3 %copy.38 = bf16[64,8,128,128]{3,2,1,0:T(8,128)(2,1)} copy(bf16[64,8,128,128]{3,1,2,0:T(8,128)(2,1)S(1)} %bitcast.81) | data formatting | bytes 33554432 | tf_op jit(solution)/shard_map/while
  157.8 6.9 %convolution_convert_fusion.4 = bf16[8,64,16384]{2,1,0:T(8,128)(2,1)S(1)} fusion(bf16[128,16384]{1,0:T(8,128)(2,1)} %get-tuple-element.174, s32[8,64]{1,0:T(8,128)S(1)} %get-tuple-element.150), kind=kOutput, calls=%fused_computation.3.clone.1 | convolution fusion | flops 2155937792 | bytes 20973568 | tf_op jit(solution)/shard_map/while/body/eval_jaxpr/nkm,mx->nkx/dot_general | solution.py:34
  164.7 8.3 %copy.37 = bf16[64,8,128,128]{3,2,1,0:T(8,128)(2,1)} copy(bf16[64,8,128,128]{3,1,2,0:T(8,128)(2,1)S(1)} %bitcast.82) | data formatting | bytes 33554432 | tf_op jit(solution)/shard_map/while
  173.0 13.3 %fusion.30 = f32[4,8,128,128]{3,2,1,0:T(8,128)} fusion(f32[4,8,128,128]{3,2,1,0:T(8,128)} %get-tuple-element.161, s32[]{:T(128)} %get-tuple-element.160, bf16[8,64,128,128]{3,2,1,0:T(8,128)(2,1)} %bitcast.84, bf16[8,64,128,128]{3,2,1,0:T(8,128)(2,1)} %bitcast.83), kind=kOutput, calls=%fused_computation.11.clone.1 | convolution fusion | flops 2147483648 | bytes 34079232 | tf_op jit(solution)/shard_map/while/body/eval_jaxpr/nkpc,nkqc->npq/dot_general | solution.py:39
  186.3 0.7 dynamic-slice_bitcast_fusion.5
  187.1 7.0 %convolution_convert_fusion.5 = bf16[8,64,16384]{2,1,0:T(8,128)(2,1)S(1)} fusion(bf16[128,16384]{1,0:T(8,128)(2,1)} %get-tuple-element.172, s32[8,64]{1,0:T(8,128)S(1)} %get-tuple-element.151, pred[8,64]{1,0:T(8,128)(4,1)S(1)} %dynamic-slice_bitcast_fusion.6), kind=kOutput, calls=%fused_computation.4.clone.1 | convolution fusion | flops 2156003328 | bytes 20974080 | tf_op jit(solution)/shard_map/while/body/eval_jaxpr/nkm,mx->nkx/dot_general | solution.py:31
  194.0 8.3 %copy.38 = bf16[64,8,128,128]{3,2,1,0:T(8,128)(2,1)} copy(bf16[64,8,128,128]{3,1,2,0:T(8,128)(2,1)S(1)} %bitcast.81) | data formatting | bytes 33554432 | tf_op jit(solution)/shard_map/while
  202.3 6.9 %convolution_convert_fusion.4 = bf16[8,64,16384]{2,1,0:T(8,128)(2,1)S(1)} fusion(bf16[128,16384]{1,0:T(8,128)(2,1)} %get-tuple-element.174, s32[8,64]{1,0:T(8,128)S(1)} %get-tuple-element.150), kind=kOutput, calls=%fused_computation.3.clone.1 | convolution fusion | flops 2155937792 | bytes 20973568 | tf_op jit(solution)/shard_map/while/body/eval_jaxpr/nkm,mx->nkx/dot_general | solution.py:34
  209.3 8.3 %copy.37 = bf16[64,8,128,128]{3,2,1,0:T(8,128)(2,1)} copy(bf16[64,8,128,128]{3,1,2,0:T(8,128)(2,1)S(1)} %bitcast.82) | data formatting | bytes 33554432 | tf_op jit(solution)/shard_map/while
  217.6 13.3 %fusion.30 = f32[4,8,128,128]{3,2,1,0:T(8,128)} fusion(f32[4,8,128,128]{3,2,1,0:T(8,128)} %get-tuple-element.161, s32[]{:T(128)} %get-tuple-element.160, bf16[8,64,128,128]{3,2,1,0:T(8,128)(2,1)} %bitcast.84, bf16[8,64,128,128]{3,2,1,0:T(8,128)(2,1)} %bitcast.83), kind=kOutput, calls=%fused_computation.11.clone.1 | convolution fusion | flops 2147483648 | bytes 34079232 | tf_op jit(solution)/shard_map/while/body/eval_jaxpr/nkpc,nkqc->npq/dot_general | solution.py:39
  230.9 0.7 dynamic-slice_bitcast_fusion.5
  231.6 7.0 %convolution_convert_fusion.5 = bf16[8,64,16384]{2,1,0:T(8,128)(2,1)S(1)} fusion(bf16[128,16384]{1,0:T(8,128)(2,1)} %get-tuple-element.172, s32[8,64]{1,0:T(8,128)S(1)} %get-tuple-element.151, pred[8,64]{1,0:T(8,128)(4,1)S(1)} %dynamic-slice_bitcast_fusion.6), kind=kOutput, calls=%fused_computation.4.clone.1 | convolution fusion | flops 2156003328 | bytes 20974080 | tf_op jit(solution)/shard_map/while/body/eval_jaxpr/nkm,mx->nkx/dot_general | solution.py:31
  238.6 8.3 %copy.38 = bf16[64,8,128,128]{3,2,1,0:T(8,128)(2,1)} copy(bf16[64,8,128,128]{3,1,2,0:T(8,128)(2,1)S(1)} %bitcast.81) | data formatting | bytes 33554432 | tf_op jit(solution)/shard_map/while
  246.8 6.9 %convolution_convert_fusion.4 = bf16[8,64,16384]{2,1,0:T(8,128)(2,1)S(1)} fusion(bf16[128,16384]{1,0:T(8,128)(2,1)} %get-tuple-element.174, s32[8,64]{1,0:T(8,128)S(1)} %get-tuple-element.150), kind=kOutput, calls=%fused_computation.3.clone.1 | convolution fusion | flops 2155937792 | bytes 20973568 | tf_op jit(solution)/shard_map/while/body/eval_jaxpr/nkm,mx->nkx/dot_general | solution.py:34
  253.8 8.3 %copy.37 = bf16[64,8,128,128]{3,2,1,0:T(8,128)(2,1)} copy(bf16[64,8,128,128]{3,1,2,0:T(8,128)(2,1)S(1)} %bitcast.82) | data formatting | bytes 33554432 | tf_op jit(solution)/shard_map/while
  262.1 13.3 %fusion.30 = f32[4,8,128,128]{3,2,1,0:T(8,128)} fusion(f32[4,8,128,128]{3,2,1,0:T(8,128)} %get-tuple-element.161, s32[]{:T(128)} %get-tuple-element.160, bf16[8,64,128,128]{3,2,1,0:T(8,128)(2,1)} %bitcast.84, bf16[8,64,128,128]{3,2,1,0:T(8,128)(2,1)} %bitcast.83), kind=kOutput, calls=%fused_computation.11.clone.1 | convolution fusion | flops 2147483648 | bytes 34079232 | tf_op jit(solution)/shard_map/while/body/eval_jaxpr/nkpc,nkqc->npq/dot_general | solution.py:39
  275.4 0.7 dynamic-slice_bitcast_fusion.5
  276.1 7.0 %convolution_convert_fusion.5 = bf16[8,64,16384]{2,1,0:T(8,128)(2,1)S(1)} fusion(bf16[128,16384]{1,0:T(8,128)(2,1)} %get-tuple-element.172, s32[8,64]{1,0:T(8,128)S(1)} %get-tuple-element.151, pred[8,64]{1,0:T(8,128)(4,1)S(1)} %dynamic-slice_bitcast_fusion.6), kind=kOutput, calls=%fused_computation.4.clone.1 | convolution fusion | flops 2156003328 | bytes 20974080 | tf_op jit(solution)/shard_map/while/body/eval_jaxpr/nkm,mx->nkx/dot_general | solution.py:31
  283.1 8.3 %copy.38 = bf16[64,8,128,128]{3,2,1,0:T(8,128)(2,1)} copy(bf16[64,8,128,128]{3,1,2,0:T(8,128)(2,1)S(1)} %bitcast.81) | data formatting | bytes 33554432 | tf_op jit(solution)/shard_map/while
  291.4 6.9 %convolution_convert_fusion.4 = bf16[8,64,16384]{2,1,0:T(8,128)(2,1)S(1)} fusion(bf16[128,16384]{1,0:T(8,128)(2,1)} %get-tuple-element.174, s32[8,64]{1,0:T(8,128)S(1)} %get-tuple-element.150), kind=kOutput, calls=%fused_computation.3.clone.1 | convolution fusion | flops 2155937792 | bytes 20973568 | tf_op jit(solution)/shard_map/while/body/eval_jaxpr/nkm,mx->nkx/dot_general | solution.py:34
  298.3 8.3 %copy.37 = bf16[64,8,128,128]{3,2,1,0:T(8,128)(2,1)} copy(bf16[64,8,128,128]{3,1,2,0:T(8,128)(2,1)S(1)} %bitcast.82) | data formatting | bytes 33554432 | tf_op jit(solution)/shard_map/while
  306.6 13.3 %fusion.30 = f32[4,8,128,128]{3,2,1,0:T(8,128)} fusion(f32[4,8,128,128]{3,2,1,0:T(8,128)} %get-tuple-element.161, s32[]{:T(128)} %get-tuple-element.160, bf16[8,64,128,128]{3,2,1,0:T(8,128)(2,1)} %bitcast.84, bf16[8,64,128,128]{3,2,1,0:T(8,128)(2,1)} %bitcast.83), kind=kOutput, calls=%fused_computation.11.clone.1 | convolution fusion | flops 2147483648 | bytes 34079232 | tf_op jit(solution)/shard_map/while/body/eval_jaxpr/nkpc,nkqc->npq/dot_general | solution.py:39
  320.0 71.5 %all-reduce.2.cloned.1.call-done = f32[32,128,128]{2,1,0:T(8,128)} async-done(((f32[32,128,128]{2,1,0:T(8,128)}), f32[32,128,128]{2,1,0:T(8,128)}) %all-reduce.2.cloned.1.call-update) | async-done | bytes 2097168 | tf_op jit(solution)/shard_map/psum | solution.py:66
  391.5 1.7 constant_dynamic-slice_fusion
  (23 shorter events, 0.2 us)
Async XLA Ops:
  6.5 16.1 %copy-start = (bf16[64,128,128]{2,1,0:T(8,128)(2,1)S(1)}, bf16[64,128,128]{2,1,0:T(8,128)(2,1)}, u32[]{:S(2)}) copy-start(bf16[64,128,128]{2,1,0:T(8,128)(2,1)} %param.9) | copy-start | bytes 6291460
  32.5 5.0 %copy-start.2 = (bf16[64,128,128]{2,1,0:T(8,128)(2,1)S(1)}, bf16[64,128,128]{2,1,0:T(8,128)(2,1)}, u32[]{:S(2)}) copy-start(bf16[64,128,128]{2,1,0:T(8,128)(2,1)} %param.8) | copy-start | bytes 6291460
  32.5 56.5 %all-to-all-start.2 = ((bf16[16,8,128,128]{3,1,2,0:T(8,128)(2,1)}), bf16[16,8,128,128]{3,1,2,0:T(8,128)(2,1)}, u32[]{:S(2)}, u32[]{:S(2)}) async-start(bf16[16,8,128,128]{3,1,2,0:T(8,128)(2,1)} %copy_select_fusion), calls=%async_computation.2 | async-start | bytes 8388608 | tf_op jit(solution)/shard_map/all_to_all | solution.py:57
  47.4 47.9 %copy-start.3 = (s32[32,1]{0,1:T(1,128)S(1)}, s32[32,1]{0,1:T(1,128)}, u32[]{:S(2)}) copy-start(s32[32,1]{0,1:T(1,128)} %param.13) | copy-start | bytes 388
  89.0 52.8 %all-to-all-start.1 = ((bf16[16,8,128,128]{3,1,2,0:T(8,128)(2,1)}), bf16[16,8,128,128]{3,1,2,0:T(8,128)(2,1)}, u32[]{:S(2)}, u32[]{:S(2)}) async-start(bf16[16,8,128,128]{3,1,2,0:T(8,128)(2,1)} %copy_select_fusion.1), calls=%async_computation.1 | async-start | bytes 8388608 | tf_op jit(solution)/shard_map/all_to_all | solution.py:56
  94.5 297.0 %all-reduce.2.cloned.1.call-start = ((), (), s32[]{:S(2)}) async-start(), calls=%async_computation.3 | async-start | bytes 4194304 | tf_op jit(solution)/shard_map/psum | solution.py:66
  320.0 73.2 %copy-start.1 = (bf16[64,128,128]{2,1,0:T(8,128)(2,1)S(1)}, bf16[64,128,128]{2,1,0:T(8,128)(2,1)}, u32[]{:S(2)}) copy-start(bf16[64,128,128]{2,1,0:T(8,128)(2,1)} %param.9) | copy-start | bytes 6291460
Sparse Core Ops, SparseCore 0:
  320.1 71.3 all-reduce.1
where the time goes:
time: 402 us; the launch traced here: 400 us
  waiting for transfers between devices  159 us (40%)
  matrix products  109 us (27%)
  local copies, waits for them, and re-layouts  79 us (20%)
  blocking collectives  14.8 us (4%)
  other arithmetic  14.4 us (4%)
  between operations  13.5 us (3%)
  starting transfers between devices  10.4 us (3%)
    psum x1, waiting for transfers between devices, body(): total_sum = lax.psum(partial_sum, 'red')  71.5 us
    while x8, local copies, waits for them, and re-layouts  66.3 us
    dot_general x4, matrix products, one_block(): jnp.einsum('nkpc,nkqc->npq', left_tiles, right_tiles, preferred_element_t...  53.3 us
    all_to_all x1, waiting for transfers between devices, body(): lax.all_to_all(send_amp, 'own', split_axis=0, concat_axis=0, tiled=True)  45.7 us
    all_to_all x1, waiting for transfers between devices, body(): lax.all_to_all(send_int, 'own', split_axis=0, concat_axis=0, tiled=True)  41.6 us
    dot_general x4, matrix products, one_block(): jnp.einsum('nkm,mx->nkx', pick_amp, flat_amp, preferred_element_type=jnp....  27.9 us
    dot_general x4, matrix products, one_block(): jnp.einsum('nkm,mx->nkx', pick_int, flat_int, preferred_element_type=jnp....  27.8 us
    all_to_all x1, blocking collectives, body(): lax.all_to_all(wanted, 'own', split_axis=0, concat_axis=0, tiled=True)  14.8 us
  transfers between devices with their start and end apart: 3, of which 3 were waited for; matrix products, arithmetic and copies ran while one was open for 3% of the time, Pallas kernels for 0%

commit v1 on v0

v1 whole, which is shorter than its diff:
```python
import functools

import jax
import jax.numpy as jnp
from jax import lax
from jax.experimental import pallas as pl
from jax.experimental.pallas import tpu as pltpu
from jax.sharding import PartitionSpec as P

GROUP = 4


def pack_body(lists, asked, *refs):
    stores, out, sem = refs[:-2], refs[-2], refs[-1]
    peers, slots = out.shape[0], out.shape[1]
    cap = asked.shape[1] // 2
    last = stores[0].shape[0] - 1

    def one_peer(peer, carry):
        for pos, (which, kind, slot) in enumerate(lists):
            tile = jnp.clip(asked[peer, kind * cap + slot], 0, last)
            pltpu.make_async_copy(stores[which].at[tile], out.at[peer, pos], sem).start()
        return carry

    lax.fori_loop(0, peers, one_peer, 0)
    pltpu.make_async_copy(out, out, sem).wait()


def pack(lists, asked, stores):
    peers = asked.shape[0]
    tile = stores[0].shape[1:]
    return pl.pallas_call(
        functools.partial(pack_body, lists),
        in_specs=[pl.BlockSpec(memory_space=pltpu.SMEM)] + [pl.BlockSpec(memory_space=pl.ANY)] * len(stores),
        out_specs=pl.BlockSpec(memory_space=pl.ANY),
        out_shape=jax.ShapeDtypeStruct((peers, len(lists)) + tile, stores[0].dtype),
        scratch_shapes=[pltpu.SemaphoreType.DMA(())],
    )(asked, *stores)


def row_sum(row, start, stop, left_at, right_at, left_buf, right_buf, zero_slot, acc):
    groups = (stop - start + GROUP - 1) // GROUP

    def one_group(g, acc):
        base = start + g * GROUP
        lefts, rights = [], []
        for j in range(GROUP):
            pos = base + j
            left = jnp.where(pos < stop, left_at[row, pos], zero_slot)
            lefts.append(left_buf[left])
            rights.append(right_buf[right_at[row, pos]])
        return acc + lax.dot_general(
            jnp.concatenate(lefts, axis=1),
            jnp.concatenate(rights, axis=1),
            (((1,), (1,)), ((), ())),
            preferred_element_type=jnp.float32,
        )

    return lax.fori_loop(0, groups, one_group, acc)


def first_body(left_at, right_at, low, got, out, buf, sem):
    copy = pltpu.make_async_copy(got, buf.at[pl.ds(0, got.shape[0])], sem)
    copy.start()
    zero_slot = got.shape[0]
    buf[zero_slot] = jnp.zeros(buf.shape[1:], buf.dtype)
    copy.wait()

    def one_row(row, carry):
        out[row] = row_sum(row, 0, low[row], left_at, right_at, buf, buf, zero_slot, jnp.zeros(out.shape[1:], out.dtype))
        return carry

    lax.fori_loop(0, out.shape[0], one_row, 0)


def second_body(left_at, right_at, low, live, place, got, rest, before, out, left_buf, right_buf, acc_buf, sems):
    holders, cap = left_buf.shape[0] - 1, left_buf.shape[1]
    copies = [
        pltpu.make_async_copy(before, acc_buf, sems.at[0]),
        pltpu.make_async_copy(got.at[:, pl.ds(0, cap)], left_buf.at[pl.ds(0, holders)], sems.at[1]),
        pltpu.make_async_copy(rest, right_buf, sems.at[2]),
    ]
    for copy in copies:
        copy.start()
    left_buf[holders, 0] = jnp.zeros(left_buf.shape[2:], left_buf.dtype)
    for copy in copies:
        copy.wait()
    flat_left = left_buf.reshape((holders + 1) * cap, left_buf.shape[2], left_buf.shape[3])
    zero_slot = holders * cap
    half, steps, share = out.shape[0], out.shape[1], out.shape[2]

    def one_out(i, carry):
        side = i // (steps * share)
        step = (i // share) % steps
        j = i % share
        core = jnp.where(side == 0, 1 - place[1], place[1])
        row = (((place[0] + step) % steps) * half + core) * share + j
        out[side, step, j] = row_sum(
            row, low[row], live[row], left_at, right_at, flat_left, right_buf, zero_slot, acc_buf[row]
        )
        return carry

    lax.fori_loop(0, half * steps * share, one_out, 0)


def body(amp_tiles, int_tiles, requests, tri_amp, tri_int, tri_count):
    wanted = requests[0, 0]
    peers, kinds, cap = wanted.shape
    rows, slots = tri_amp.shape[0], tri_amp.shape[2]
    tile = amp_tiles.shape[1:]
    cut = cap // 2
    red = lax.axis_size("red")
    share = rows // red
    me = lax.axis_index("red")

    asked = lax.all_to_all(wanted.reshape(peers, kinds * cap), "own", split_axis=0, concat_axis=0, tiled=True)
    first_list = tuple((0, 0, s) for s in range(cap)) + tuple((1, 1, s) for s in range(cut))
    second_list = tuple((0, 1, s) for s in range(cut, cap))
    send_first = pack(first_list, asked, (amp_tiles, int_tiles))
    got_first = lax.all_to_all(send_first, "own", split_axis=0, concat_axis=0, tiled=True)
    send_second = pack(second_list, asked, (int_tiles,))
    got_second = lax.all_to_all(send_second, "own", split_axis=0, concat_axis=0, tiled=True)

    amp_pos, int_pos = tri_amp[:, 0], tri_int[:, 0]
    count = tri_count[:, 0]
    alive = lax.broadcasted_iota(jnp.int32, (rows, slots), 1) < count[:, None]
    is_low = int_pos % cap < cut
    key = jnp.where(alive, jnp.where(is_low, 0, 1), 2)
    code = lax.sort((key * peers * cap + amp_pos) * peers * cap + int_pos, dimension=1)
    low = jnp.sum((alive & is_low).astype(jnp.int32), axis=1)
    amp_pos = (code // (peers * cap)) % (peers * cap)
    int_pos = code % (peers * cap)
    pad = ((0, 0), (0, GROUP))
    width = cap + cut
    holder, slot = int_pos // cap, int_pos % cap
    left_first = jnp.pad((amp_pos // cap) * width + amp_pos % cap, pad)
    right_first = jnp.pad(jnp.where(slot < cut, holder * width + cap + slot, 0), pad)
    left_second = jnp.pad(amp_pos, pad)
    right_second = jnp.pad(jnp.where(slot < cut, 0, holder * (cap - cut) + slot - cut), pad)

    smem = pl.BlockSpec(memory_space=pltpu.SMEM)
    anywhere = pl.BlockSpec(memory_space=pl.ANY)
    vmem = pl.BlockSpec(memory_space=pltpu.VMEM)
    params = pltpu.CompilerParams(vmem_limit_bytes=40 * 2**20)
    flat_first = got_first.reshape((-1,) + tile)
    before = pl.pallas_call(
        first_body,
        in_specs=[smem] * 3 + [anywhere],
        out_specs=vmem,
        out_shape=jax.ShapeDtypeStruct((rows,) + tile, jnp.float32),
        scratch_shapes=[pltpu.VMEM((flat_first.shape[0] + 1,) + tile, flat_first.dtype), pltpu.SemaphoreType.DMA(())],
        compiler_params=params,
    )(left_first, right_first, low, flat_first)

    place = jnp.stack([me // 2, me % 2]).astype(jnp.int32)
    flat_second = got_second.reshape((-1,) + tile)
    steps = red // 2
    part = pl.pallas_call(
        second_body,
        in_specs=[smem] * 5 + [anywhere] * 3,
        out_specs=vmem,
        out_shape=jax.ShapeDtypeStruct((2, steps, share) + tile, jnp.float32),
        scratch_shapes=[
            pltpu.VMEM((peers + 1, cap) + tile, flat_first.dtype),
            pltpu.VMEM(flat_second.shape, flat_second.dtype),
            pltpu.VMEM((rows,) + tile, jnp.float32),
            pltpu.SemaphoreType.DMA((3,)),
        ],
        compiler_params=params,
    )(left_second, right_second, low, count, place, got_first, flat_second, before)

    swapped = lax.ppermute(part[0], "red", [(i, i ^ 1) for i in range(red)])
    total = swapped[0] + part[1, 0]
    for step in [steps // 2] + [s for s in range(1, steps) if s != steps // 2]:
        block = swapped[step] + part[1, step]
        total = total + lax.ppermute(
            block, "red", [(i, ((i // 2 + step) % steps) * 2 + i % 2) for i in range(red)]
        )
    return total


def solution(mesh):
    placed = (
        P(("own", "red"), None, None),
        P(("own", "red"), None, None),
        P("own", "red", None, None, None),
        P("own", "red", None),
        P("own", "red", None),
        P("own", "red"),
    )
    return jax.shard_map(
        body, mesh=mesh, in_specs=placed, out_specs=P(("own", "red"), None, None), check_vma=False
    )
```

time: 402 us -> 422 us (1.050)
  Pallas kernels: 0 us -> 311 us
  waiting for transfers between devices: 159 us -> 44.7 us
  matrix products: 109 us -> 0 us
  local copies, waits for them, and re-layouts: 79 us -> 3.99 us
  starting transfers between devices: 10.4 us -> 42.2 us
  between operations: 13.5 us -> 0.2 us
  other arithmetic: 14.4 us -> 2.32 us
    pallas_call x0 -> x4, Pallas kernels: none -> 311 us  [the longest x2 258 us: pack(): pl.pallas_call(functools.partial(pack_body, lists), in_specs=[pl.BlockSpe...]
    dot_general x12 -> x0, matrix products: 109 us -> none  [the longest x4 53.3 us: one_block(): jnp.einsum('nkpc,nkqc->npq', left_tiles, right_tiles, preferred_element_t...]
    psum x1 -> x0, waiting for transfers between devices: 71.5 us -> none  [body(): total_sum = lax.psum(partial_sum, 'red')]
    while x8 -> x0, local copies, waits for them, and re-layouts: 66.3 us -> none
    all_to_all x2, waiting for transfers between devices: 87.3 us -> 30.2 us  [the longest x1 30.2 us: body(): lax.all_to_all(send_first, 'own', split_axis=0, concat_axis=0, tiled=True)]
    ppermute x0 -> x4, starting transfers between devices: none -> 30.4 us  [the longest x1 27.1 us: body(): swapped = lax.ppermute(part[0], 'red', [(i, i ^ 1) for i in range(red)])]
    ppermute x0 -> x4, waiting for transfers between devices: none -> 14.4 us  [the longest x3 12.2 us: body(): lax.ppermute(block, 'red', [(i, (i // 2 + step) % steps * 2 + i % 2) for...]
    select_n x4 -> x1, other arithmetic: 13.7 us -> 0.07 us  [body(): jnp.where(slot < cut, holder * width + cap + slot, 0)]
  transfers between devices with their start and end apart: 3 -> 6, of which waited for: 3 -> 4; matrix products, arithmetic and copies ran while one was open for 3% -> 0% of each run, Pallas kernels for 0% -> 25%
where the time goes in v1:
time: 422 us; the launch traced here: 419 us
  Pallas kernels  311 us (74%)
  waiting for transfers between devices  44.7 us (11%)
  starting transfers between devices  42.2 us (10%)
  blocking collectives  14.9 us (4%)
    pallas_call x2, Pallas kernels, pack(): pl.pallas_call(functools.partial(pack_body, lists), in_specs=[pl.BlockSpe...  258 us
    pallas_call x1, Pallas kernels, body(): pl.pallas_call(first_body, in_specs=[smem] * 3 + [anywhere], out_specs=vm...  37.8 us
    all_to_all x1, waiting for transfers between devices, body(): lax.all_to_all(send_first, 'own', split_axis=0, concat_axis=0, tiled=True)  30.2 us
    ppermute x1, starting transfers between devices, body(): swapped = lax.ppermute(part[0], 'red', [(i, i ^ 1) for i in range(red)])  27.1 us
    pallas_call x1, Pallas kernels, body(): pl.pallas_call(second_body, in_specs=[smem] * 5 + [anywhere] * 3, out_spe...  15.1 us
    all_to_all x1, blocking collectives, body(): lax.all_to_all(wanted.reshape(peers, kinds * cap), 'own', split_axis=0, c...  14.9 us
    ppermute x3, waiting for transfers between devices, body(): lax.ppermute(block, 'red', [(i, (i // 2 + step) % steps * 2 + i % 2) for...  12.2 us
  transfers between devices with their start and end apart: 6, of which 4 were waited for; matrix products, arithmetic and copies ran while one was open for 0% of the time, Pallas kernels for 25%

profile of v1, /device:TPU:1, one launch (start us, length us, event | category | flops | bytes accessed | tf_op | source)
XLA Modules:
  0.0 419.2 jit_solution(17832597629876363672)
XLA Ops:
  0.0 0.8 copy.19
  0.8 14.9 %all_to_all.21 = s32[16,1,16]{2,1,0:T(1,128)} all-to-all(s32[16,1,16]{2,1,0:T(1,128)S(1)} %copy.19), channel_id=1, replica_groups=mesh['own'=16,'red'=8] {'own'}, dimensions={0} | all-to-all | bytes 2048 | tf_op jit(solution)/shard_map/all_to_all | solution.py:116
  15.7 192.5 %shard_map.64 = bf16[16,12,128,128]{3,2,1,0:T(8,128)(2,1)} custom-call(s32[16,16]{1,0:T(8,128)} %bitcast.53, bf16[64,128,128]{2,1,0:T(8,128)(2,1)} %refs_0_.2, bf16[64,128,128]{2,1,0:T(8,128)(2,1)} %refs_0_.3), custom_call_target="tpu_custom_call" | custom-call | tf_op jit(solution)/shard_map/pallas_call | solution.py:32
  208.2 4.6 %all-to-all-start.1 = ((bf16[16,12,128,128]{3,2,1,0:T(8,128)(2,1)}), bf16[16,12,128,128]{3,2,1,0:T(8,128)(2,1)}, u32[]{:S(2)}, u32[]{:S(2)}) async-start(bf16[16,12,128,128]{3,2,1,0:T(8,128)(2,1)} %shard_map.64), calls=%async_computation.1 | async-start | bytes 12582912 | tf_op jit(solution)/shard_map/all_to_all | solution.py:120
  212.8 65.4 %shard_map.65 = bf16[16,4,128,128]{3,2,1,0:T(8,128)(2,1)} custom-call(s32[16,16]{1,0:T(8,128)} %bitcast.54, bf16[64,128,128]{2,1,0:T(8,128)(2,1)} %refs_0_.3), custom_call_target="tpu_custom_call" | custom-call | tf_op jit(solution)/shard_map/pallas_call | solution.py:32
  278.3 0.0 copy-start.2
  278.3 0.0 copy-start.3
  278.3 0.0 copy-start.4
  278.3 30.2 %all-to-all-done.1.got = bf16[16,12,128,128]{3,2,1,0:T(8,128)(2,1)} async-done(((bf16[16,12,128,128]{3,2,1,0:T(8,128)(2,1)}), bf16[16,12,128,128]{3,2,1,0:T(8,128)(2,1)}, u32[]{:S(2)}, u32[]{:S(2)}) %all-to-all-start.1) | async-done | bytes 6291488 | tf_op jit(solution)/shard_map/all_to_all | solution.py:120
  308.6 7.2 %all-to-all-start.2 = ((bf16[16,4,128,128]{3,2,1,0:T(8,128)(2,1)}), bf16[16,4,128,128]{3,2,1,0:T(8,128)(2,1)S(1)}, u32[]{:S(2)}, u32[]{:S(2)}) async-start(bf16[16,4,128,128]{3,2,1,0:T(8,128)(2,1)} %shard_map.65), calls=%async_computation.2 | async-start | bytes 4194304 | tf_op jit(solution)/shard_map/all_to_all | solution.py:122
  315.8 0.0 copy-done.2
  315.8 0.0 copy-done.3
  315.8 0.2 convert_reduce_fusion
  316.0 0.0 copy-done.4
  316.0 0.1 multiply_add_fusion
  316.1 0.1 copy.14
  316.2 1.0 sort.14
  317.2 0.1 copy.15
  317.2 0.1 add_select_fusion.8
  317.4 0.1 pad_add_fusion.place
  317.5 37.8 %shard_map.66.before = f32[32,128,128]{2,1,0:T(8,128)S(1)} custom-call(s32[32,68]{1,0:T(8,128)S(1)} %pad.15.left_at, s32[32,68]{1,0:T(8,128)S(1)} %pad.16.right_at, s32[32]{0:T(128)S(1)} %get-tuple-element.10.low, bf16[192,128,128]{2,1,0:T(8,128)(2,1)} %bitcast.8.got), custom_call_target="tpu_custom_call" | custom-call | tf_op jit(solution)/shard_map/pallas_call | solution.py:146
  355.3 0.0 copy-start
  355.3 1.3 copy-done
  356.6 0.0 all-to-all-done.2
  356.6 0.0 copy-start.1
  356.6 1.6 copy-done.1
  358.2 15.1 %shard_map.67 = f32[2,4,4,128,128]{4,3,2,1,0:T(8,128)S(1)} custom-call(s32[32,68]{1,0:T(8,128)S(1)} %pad.13.left_at, s32[32,68]{1,0:T(8,128)S(1)} %pad.14.right_at, s32[32]{0:T(128)S(1)} %get-tuple-element.10.low, s32[32]{0:T(128)S(1)} %bitcast.52, s32[2]{0:T(128)S(1)} %pad_add_fusion.place, bf16[16,12,128,128]{3,2,1,0:T(8,128)(2,1)} %all-to-all-done.1.got, ...), custom_call_target="tpu_custom_call" | custom-call | tf_op jit(solution)/shard_map/pallas_call | solution.py:158
  373.4 0.1 slice_bitcast_fusion
  373.5 27.1 %collective-permute-start = (f32[4,4,128,128]{3,2,1,0:T(8,128)S(1)}, f32[4,4,128,128]{3,2,1,0:T(8,128)S(1)}, u32[]{:S(2)}, u32[]{:S(2)}) collective-permute-start(f32[4,4,128,128]{3,2,1,0:T(8,128)S(1)} %slice_bitcast_fusion), channel_id=1, source_target_pairs={{0,1},{1,0},{2,3},{3,2},{4,5},{5,4},{6,7},{7,6},{8,9},{9,8},{10,11... | collective-permute-start | bytes 3145736 | tf_op jit(solution)/shard_map/ppermute | solution.py:172
  400.6 2.3 collective-permute-done
  402.9 0.1 fusion.2
  403.0 0.1 collective-permute-start.1
  403.1 0.9 collective-permute-start.2
  404.0 2.3 collective-permute-start.3
  406.3 5.8 %collective-permute-done.1 = f32[4,128,128]{2,1,0:T(8,128)S(1)} collective-permute-done((f32[4,128,128]{2,1,0:T(8,128)S(1)}, f32[4,128,128]{2,1,0:T(8,128)S(1)}, u32[]{:S(2)}, u32[]{:S(2)}) %collective-permute-start.1) | collective-permute-done | bytes 262176 | tf_op jit(solution)/shard_map/ppermute | solution.py:176
  412.1 6.3 %collective-permute-done.2 = f32[4,128,128]{2,1,0:T(8,128)S(1)} collective-permute-done((f32[4,128,128]{2,1,0:T(8,128)S(1)}, f32[4,128,128]{2,1,0:T(8,128)S(1)}, u32[]{:S(2)}, u32[]{:S(2)}) %collective-permute-start.2) | collective-permute-done | bytes 262176 | tf_op jit(solution)/shard_map/ppermute | solution.py:176
  418.4 0.0 collective-permute-done.3
  418.4 0.8 fusion.6
  (5 shorter events, 0.0 us)
Async XLA Ops:
  208.2 100.4 %all-to-all-start.1 = ((bf16[16,12,128,128]{3,2,1,0:T(8,128)(2,1)}), bf16[16,12,128,128]{3,2,1,0:T(8,128)(2,1)}, u32[]{:S(2)}, u32[]{:S(2)}) async-start(bf16[16,12,128,128]{3,2,1,0:T(8,128)(2,1)} %shard_map.64), calls=%async_computation.1 | async-start | bytes 12582912 | tf_op jit(solution)/shard_map/all_to_all | solution.py:120
  278.3 37.5 %copy-start.2 = (s32[32,1]{0,1:T(1,128)S(1)}, s32[32,1]{0,1:T(1,128)}, u32[]{:S(2)}) copy-start(s32[32,1]{0,1:T(1,128)} %param.11) | copy-start | bytes 388
  278.3 37.5 %copy-start.3 = (s32[32,1,64]{2,1,0:T(1,128)S(1)}, s32[32,1,64]{2,1,0:T(1,128)}, u32[]{:S(2)}) copy-start(s32[32,1,64]{2,1,0:T(1,128)} %param.10) | copy-start | bytes 24580
  278.3 37.7 %copy-start.4 = (s32[32,1,64]{2,1,0:T(1,128)S(1)}, s32[32,1,64]{2,1,0:T(1,128)}, u32[]{:S(2)}) copy-start(s32[32,1,64]{2,1,0:T(1,128)} %param.9) | copy-start | bytes 24580
  308.6 48.1 %all-to-all-start.2 = ((bf16[16,4,128,128]{3,2,1,0:T(8,128)(2,1)}), bf16[16,4,128,128]{3,2,1,0:T(8,128)(2,1)S(1)}, u32[]{:S(2)}, u32[]{:S(2)}) async-start(bf16[16,4,128,128]{3,2,1,0:T(8,128)(2,1)} %shard_map.65), calls=%async_computation.2 | async-start | bytes 4194304 | tf_op jit(solution)/shard_map/all_to_all | solution.py:122
  355.3 1.4 copy-start
  356.6 1.6 copy-start.1
  373.5 29.4 %collective-permute-start = (f32[4,4,128,128]{3,2,1,0:T(8,128)S(1)}, f32[4,4,128,128]{3,2,1,0:T(8,128)S(1)}, u32[]{:S(2)}, u32[]{:S(2)}) collective-permute-start(f32[4,4,128,128]{3,2,1,0:T(8,128)S(1)} %slice_bitcast_fusion), channel_id=1, source_target_pairs={{0,1},{1,0},{2,3},{3,2},{4,5},{5,4},{6,7},{7,6},{8,9},{9,8},{10,11... | collective-permute-start | bytes 3145736 | tf_op jit(solution)/shard_map/ppermute | solution.py:172
  403.0 9.1 %collective-permute-start.1 = (f32[4,128,128]{2,1,0:T(8,128)S(1)}, f32[4,128,128]{2,1,0:T(8,128)S(1)}, u32[]{:S(2)}, u32[]{:S(2)}) collective-permute-start(f32[4,128,128]{2,1,0:T(8,128)S(1)} %get-tuple-element.12), channel_id=1, source_target_pairs={{0,4},{1,5},{2,6},{3,7},{4,0},{5,1},{6,2},{7,3},{8,12},{9,13},{10,... | collective-permute-start | bytes 786440 | tf_op jit(solution)/shard_map/ppermute | solution.py:176
  403.1 15.4 %collective-permute-start.2 = (f32[4,128,128]{2,1,0:T(8,128)S(1)}, f32[4,128,128]{2,1,0:T(8,128)S(1)}, u32[]{:S(2)}, u32[]{:S(2)}) collective-permute-start(f32[4,128,128]{2,1,0:T(8,128)S(1)} %get-tuple-element.14), channel_id=1, source_target_pairs={{0,2},{1,3},{2,4},{3,5},{4,6},{5,7},{6,0},{7,1},{8,10},{9,11},{10,... | collective-permute-start | bytes 786440 | tf_op jit(solution)/shard_map/ppermute | solution.py:176
  404.0 14.5 %collective-permute-start.3 = (f32[4,128,128]{2,1,0:T(8,128)S(1)}, f32[4,128,128]{2,1,0:T(8,128)S(1)}, u32[]{:S(2)}, u32[]{:S(2)}) collective-permute-start(f32[4,128,128]{2,1,0:T(8,128)S(1)} %get-tuple-element.13), channel_id=1, source_target_pairs={{0,6},{1,7},{2,0},{3,1},{4,2},{5,3},{6,4},{7,5},{8,14},{9,15},{10,... | collective-permute-start | bytes 786440 | tf_op jit(solution)/shard_map/ppermute | solution.py:176
